TPU v7x, 32 devices: a whole 2x2x4 slice. The times are simulated.
32 devices in a mesh: rows: 16 (over z, y, x), cols: 2 (over core).
Axes of the slice: x: 2, y: 2, z: 4, core: 2. Of those that a mesh axis runs over, the one named last changes fastest.
Arguments:
- parent_front: float32 [4096, 2048], P('rows', 'cols')
- right_sides: float32 [4096, 64], P('rows'), may hold values from -6 to 6
- child_values: float32 [1024, 1024], P('rows', 'cols'), may hold values from -6 to 6
- block_owner: int32 [256], P('rows'), may hold values from 0 to 15, as said below
- row_map: int32 [1024], P('rows'), may hold values from 0 to 255
- col_map: int32 [1024], P('cols'), may hold values from 0 to 1023, as said below
Outputs:
- updated: float32 [4096, 2048], P('rows', 'cols')
- side_coeffs: float32 [128, 64], replicated
- side_left: float32 [4096, 64], P('rows')
Inputs may be any that keep to these rules, and one draw needn't show every extreme that they name: `block_owner`: for every k, entries k * 16 to (k + 1) * 16 - 1 form a permutation of 0 to 15. `col_map`: each aligned run of 512 entries is strictly increasing, starts with 0 and ends with 1023.
All inputs are finite; a program needn't handle non-finite values.
Results may differ from a plain program's by a relative error of at most 0.0003.
Values sent between devices are 32-bit elements; how exact they have to be, the bound alone decides.
A program may use at most 64 MiB of HBM per device.

v0:
```python
import functools

import jax
import jax.numpy as jnp
from jax import lax
from jax.experimental import pallas as pl
from jax.experimental.pallas import tpu as pltpu
from jax.sharding import PartitionSpec as P

PANEL = 128
LANES = 128
SUBLANES = 8
TILE = 256
VMEM_LIMIT = 67043328
MESH = pl.DeviceIdType.MESH
f32 = jnp.float32
bf16 = jnp.bfloat16


def pieces(value):
    first = value.astype(bf16)
    rest = value - first.astype(f32)
    second = rest.astype(bf16)
    third = (rest - second.astype(f32)).astype(bf16)
    return first, second, third


def dot(left, right, dims, precision=None):
    return lax.dot_general(left, right, (dims, ((), ())), precision=precision, preferred_element_type=f32)


def dot_full(left, right, dims=((1,), (0,))):
    return dot(left, right, dims, lax.Precision.HIGHEST)


def inverse_pair(a, b, d):
    ia = 1.0 / a
    ratio = b * ia
    i11 = 1.0 / (d - b * ratio)
    i01 = -ratio * i11
    return ia - ratio * i01, i01, i11


def sweep_four(mat, k, lane):
    cols = [mat[:, k + j : k + j + 1] for j in range(4)]
    rows = [mat[k + j : k + j + 1, :] for j in range(4)]
    d = [[jnp.broadcast_to(mat[k + i : k + i + 1, k + j : k + j + 1], (1, mat.shape[1])) for j in range(i + 1)] for i in range(4)]
    a00, a01, a11 = inverse_pair(d[0][0], d[1][0], d[1][1])
    l20, l21 = d[2][0] * a00 + d[2][1] * a01, d[2][0] * a01 + d[2][1] * a11
    l30, l31 = d[3][0] * a00 + d[3][1] * a01, d[3][0] * a01 + d[3][1] * a11
    s22 = d[2][2] - (l20 * d[2][0] + l21 * d[2][1])
    s32 = d[3][2] - (l30 * d[2][0] + l31 * d[2][1])
    s33 = d[3][3] - (l30 * d[3][0] + l31 * d[3][1])
    e22, e32, e33 = inverse_pair(s22, s32, s33)
    e20, e21 = -(e22 * l20 + e32 * l30), -(e22 * l21 + e32 * l31)
    e30, e31 = -(e32 * l20 + e33 * l30), -(e32 * l21 + e33 * l31)
    e00 = a00 - (l20 * e20 + l30 * e30)
    e10 = a01 - (l21 * e20 + l31 * e30)
    e11 = a11 - (l21 * e21 + l31 * e31)
    e = [[e00, e10, e20, e30], [e10, e11, e21, e31], [e20, e21, e22, e32], [e30, e31, e32, e33]]
    lane_row = lane[:1]
    tops = []
    for i in range(4):
        top = (e[i][0] * rows[0] + e[i][1] * rows[1]) + (e[i][2] * rows[2] + e[i][3] * rows[3])
        for j in range(4):
            top = jnp.where(lane_row == k + j, -e[i][j], top)
        tops.append(top)
    out = jnp.where((lane >= k) & (lane < k + 4), 0.0, mat)
    out = out - ((cols[0] * tops[0] + cols[1] * tops[1]) + (cols[2] * tops[2] + cols[3] * tops[3]))
    head = out[:SUBLANES]
    sub = lax.broadcasted_iota(jnp.int32, head.shape, 0)
    for j in range(4):
        head = jnp.where(sub == k + j, tops[j], head)
    return jnp.concatenate([head, out[SUBLANES:]], axis=0)


def sweep_groups(mat, count):
    size = mat.shape[0]
    lane = lax.broadcasted_iota(jnp.int32, mat.shape, 1)

    def group(_, mat):
        for k in range(0, SUBLANES, 4):
            mat = sweep_four(mat, k, lane)
        mat = jnp.concatenate([mat[SUBLANES:], mat[:SUBLANES]], axis=0)
        return pltpu.roll(mat, size - SUBLANES, 1)

    return lax.fori_loop(0, count, group, mat)


def plan(n, width):
    levels = n.bit_length() - 1
    halving = min(levels, (PANEL // SUBLANES).bit_length() - 1)
    nparts = min(3, levels)
    tiles = width // LANES
    starts = [tiles * q // nparts * LANES for q in range(nparts + 1)]
    orders = [[(q + t) % nparts for t in range(nparts)] + list(range(nparts, levels)) for q in range(nparts)]
    single = max(halving - 2, 0)
    cuts = [(t, t + 1) for t in range(single)] + [(single, halving)]
    parts = [([order[a:b] for a, b in cuts], [[bit] for bit in order[halving:]]) for order in orders]
    return starts, parts, halving


def slots_of(n):
    levels = n.bit_length() - 1
    halving = min(levels, (PANEL // SUBLANES).bit_length() - 1)
    rows, count = 0, 0
    single = max(halving - 2, 0)
    size = PANEL
    for bits in [1] * single + [halving - single]:
        size >>= bits
        rows += ((1 << bits) - 1) * size
        count += (1 << bits) - 1
    rows += (levels - halving) * SUBLANES
    count += levels - halving
    return rows, count


def kernel(n, ncols, owner_hbm, parent, rhs_hbm, child_hbm, row_map_hbm, col_map_hbm,
           front_out, panel_out, coefs_out, side_out, front, panel, coefs, side, out_sem, owner, rhs_t, row_map, col_map, child, send, recv, flat, hot, sides, prod, total, halves, gram, gram_in, gram_all,
           in_sem, a2a_send, a2a_recv, pan_send, pan_recv, gram_send, gram_recv, red_send, red_recv):
    row, col = lax.axis_index("rows"), lax.axis_index("cols")
    rows_dev, cols_dev = front.shape
    child_rows, child_cols = child.shape
    nrhs = rhs_t.shape[0]
    block = child_rows // n
    first_loads = [
        pltpu.make_async_copy(source, target, in_sem.at[k])
        for k, (source, target) in enumerate([(owner_hbm, owner), (row_map_hbm, row_map), (child_hbm, child)])
    ]
    later_loads = [
        pltpu.make_async_copy(source, target, in_sem.at[3 + k])
        for k, (source, target) in enumerate([(col_map_hbm, col_map), (rhs_hbm, rhs_t), (parent, front)])
    ]
    for load in first_loads + later_loads:
        load.start()

    barrier = pltpu.get_barrier_semaphore()
    for step in range(1, n):
        pl.semaphore_signal(barrier, inc=1, device_id=(lax.rem(row + step, n), col), device_id_type=MESH)
    for step in range(1, ncols):
        pl.semaphore_signal(barrier, inc=1, device_id=(row, lax.rem(col + step, ncols)), device_id_type=MESH)

    for load in first_loads:
        load.wait()
    source = lax.broadcasted_iota(jnp.int32, (1, child_rows), 1)
    target = jnp.zeros((1, child_rows), jnp.int32)
    for k in range(n):
        target = jnp.where(source // block == k, owner[k] * block + source % block, target)
    place = lax.broadcasted_iota(jnp.int32, (child_rows, child_rows), 0) == target
    place_f = jnp.where(place, 1.0, 0.0).astype(f32)
    landing = jnp.sum(place_f * row_map[...].astype(f32), axis=1, keepdims=True)
    place_b = place_f.astype(bf16)
    one, two, three = pieces(child[...])
    ordered = dot(place_b, one, ((1,), (0,))) + dot(place_b, two, ((1,), (0,))) + dot(place_b, three, ((1,), (0,)))
    landing = jnp.broadcast_to(landing, (child_rows, LANES))
    for k in range(n):
        send[k, :, :child_cols] = ordered[k * block : (k + 1) * block]
        send[k, :, child_cols:] = landing[k * block : (k + 1) * block]

    pl.semaphore_wait(barrier, n - 1 + ncols - 1)

    copies = []
    for step in range(1, n):
        peer = lax.rem(row + step, n)
        copy = pltpu.make_async_remote_copy(
            src_ref=send.at[peer], dst_ref=recv.at[row], send_sem=a2a_send.at[step], recv_sem=a2a_recv.at[step],
            device_id=(peer, col), device_id_type=MESH)
        copy.start()
        copies.append(copy)
    recv[row] = send[row]

    for load in later_loads:
        load.wait()
    cols_at = lax.broadcasted_iota(jnp.int32, hot.shape, 0)
    hot[...] = jnp.where(cols_at == col_map[...], 1.0, 0.0).astype(f32).astype(bf16)
    padded = jnp.concatenate([rhs_t[...], jnp.zeros((sides.shape[1] - nrhs, rows_dev), f32)], axis=0)
    sides[...] = jnp.transpose(padded)
    for copy in copies:
        copy.wait()

    for k in range(n):
        flat[k * block : (k + 1) * block, :] = recv[k]
    vals = jnp.concatenate(pieces(flat[:, :child_cols]), axis=0)
    where_rows = flat[:, child_cols:].astype(jnp.int32)
    rows_at = lax.broadcasted_iota(jnp.int32, where_rows.shape, 1)
    landed = jnp.concatenate(
        [jnp.where(where_rows == rows_at + t * LANES, 1.0, 0.0).astype(f32) for t in range(rows_dev // LANES)], axis=1)
    landed3 = jnp.concatenate([landed] * 3, axis=0).astype(bf16)

    def assemble(first, last):
        spread3 = dot(vals, hot[first:last, :], ((1,), (1,)))
        spread = spread3[:child_rows] + spread3[child_rows : 2 * child_rows] + spread3[2 * child_rows :]
        stacked = jnp.concatenate(pieces(spread), axis=0)
        front[:, first:last] = front[:, first:last] + dot(landed3, stacked, ((0,), (0,)))

    assemble(0, PANEL)
    pan_copies = [
        pltpu.make_async_remote_copy(
            src_ref=front.at[:, pl.ds(0, PANEL)], dst_ref=panel, send_sem=pan_send.at[step - 1], recv_sem=pan_recv,
            device_id=(row, step), device_id_type=MESH)
        for step in range(1, ncols)
    ]

    @pl.when(col == 0)
    def _():
        for copy in pan_copies:
            copy.start()
        panel[...] = front[:, :PANEL]

    assemble(PANEL, cols_dev)

    @pl.when(col == 0)
    def _():
        for copy in pan_copies:
            copy.wait_send()

    @pl.when(col != 0)
    def _():
        pan_copies[0].wait_recv()

    block_panel = panel[...]
    trans = ((0,), (0,))
    gram[...] = dot_full(block_panel, block_panel, trans)

    chunks = min(n, PANEL // SUBLANES)
    chunk = PANEL // chunks
    own_chunk = lax.rem(row, chunks)
    own_rows = pl.ds(pl.multiple_of(own_chunk * chunk, SUBLANES), chunk)
    gathers = []
    for step in range(1, n):
        peer = lax.rem(row + step, n)
        start = pl.multiple_of(lax.rem(peer, chunks) * chunk, SUBLANES)
        copy = pltpu.make_async_remote_copy(
            src_ref=gram.at[pl.ds(start, chunk)], dst_ref=gram_in.at[row],
            send_sem=gram_send.at[step], recv_sem=gram_recv.at[step], device_id=(peer, col), device_id_type=MESH)
        copy.start()
        gathers.append(copy)
    gram_in[row] = gram[own_rows, :]

    def products(first, last):
        split = min(max(first, cols_dev), last)
        if split > first:
            prod[:, first:split] = dot_full(block_panel, front[:, first:split], trans)
        if last > split:
            prod[:, split:last] = dot_full(block_panel, sides[:, split - cols_dev : last - cols_dev], trans)

    keep_copies = [
        pltpu.make_async_copy(front, front_out, out_sem.at[0]),
        pltpu.make_async_copy(panel, panel_out, out_sem.at[1]),
    ]
    for copy in keep_copies:
        copy.start()

    starts, parts, halving = plan(n, prod.shape[1])
    base = [row * 0] * len(parts)
    nstages = len(parts[0][0])

    def own_bit(bit):
        return (row // (1 << bit)) % 2

    def members(bits):
        mine = sum(own_bit(bit) * (1 << i) for i, bit in enumerate(bits))
        others = []
        for d in range(1, 1 << len(bits)):
            code, peer = 0, row
            for i, bit in enumerate(bits):
                own = own_bit(bit)
                flip = d >> i & 1
                code = code + (1 - own if flip else own) * (1 << i)
                peer = peer + ((1 - 2 * own) * (1 << bit) if flip else 0)
            others.append((code, peer))
        return mine, others

    def send_part(q, stage, at, slot, size, split):
        groups, extras = parts[q]
        bits = groups[stage] if split else extras[stage]
        mine, others = members(bits)
        piece = size >> len(bits) if split else size
        keep = pl.multiple_of(base[q] + mine * piece if split else base[q], SUBLANES)
        width = starts[q + 1] - starts[q]
        sent = []
        for d, (code, peer) in enumerate(others):
            give = pl.multiple_of(base[q] + code * piece, SUBLANES) if split else keep
            copy = pltpu.make_async_remote_copy(
                src_ref=prod.at[pl.ds(give, piece), pl.ds(starts[q], width)],
                dst_ref=halves.at[q, pl.ds(at + d * piece, piece), pl.ds(0, width)],
                send_sem=red_send.at[q, slot + d], recv_sem=red_recv.at[q, slot + d],
                device_id=(peer, col), device_id_type=MESH)
            copy.start()
            sent.append((copy, at + d * piece))
        base[q] = keep
        return sent, keep, piece, width

    def send_stage(stage, at, slot, size, split, before):
        held = []
        for q in range(len(parts)):
            before(q)
            if split:
                marks[q].append(base[q])
            held.append(send_part(q, stage, at, slot, size, split))
        used, piece = len(held[0][0]), held[0][2]
        return held, at + used * piece, slot + used, piece

    def adder(held):
        def add_part(q):
            sent, keep, piece, width = held[q]
            for copy, _ in sent:
                copy.wait()
            spot = (pl.ds(keep, piece), slice(starts[q], starts[q + 1]))
            value = prod[spot]
            for _, at in sent:
                value = value + halves[q, at : at + piece, :width]
            prod[spot] = value

        return add_part

    def share_part(q, stage, slot, piece):
        _, others = members(parts[q][0][stage])
        keep = pl.multiple_of(base[q], SUBLANES)
        spot = total.at[pl.ds(keep, piece), pl.ds(starts[q], starts[q + 1] - starts[q])]
        sent = []
        for d, (_, peer) in enumerate(others):
            copy = pltpu.make_async_remote_copy(
                src_ref=spot, dst_ref=spot, send_sem=red_send.at[q, slot + d], recv_sem=red_recv.at[q, slot + d],
                device_id=(peer, col), device_id_type=MESH)
            copy.start()
            sent.append(copy)
        return sent

    marks = [[] for _ in parts]
    at, slot, size = 0, 0, PANEL
    held, at, slot, size = send_stage(0, at, slot, size, True, lambda q: products(starts[q], starts[q + 1]))

    for copy in gathers:
        copy.wait()
    summed = gram_in[0]
    for k in range(1, n):
        summed = summed + gram_in[k]
    gram_all[own_rows, :] = summed
    spreads = []
    for step in range(1, chunks):
        peer = row - own_chunk + lax.rem(own_chunk + step, chunks)
        copy = pltpu.make_async_remote_copy(
            src_ref=gram_all.at[own_rows], dst_ref=gram_all.at[own_rows],
            send_sem=gram_send.at[n + step], recv_sem=gram_recv.at[n + step],
            device_id=(peer, col), device_id_type=MESH)
        copy.start()
        spreads.append(copy)

    for stage in range(1, nstages):
        held, at, slot, size = send_stage(stage, at, slot, size, True, adder(held))
    for copy in spreads:
        copy.wait()
    turns = PANEL // SUBLANES
    mat, done = gram_all[...], 0

    def turn_by(mat, done, share):
        upto = min(turns, done + share)
        return (sweep_groups(mat, upto - done) if upto > done else mat), upto

    mat, done = turn_by(mat, done, 3)
    for stage in range(len(parts[0][1])):
        held, at, slot, size = send_stage(stage, at, slot, size, False, adder(held))
    last_add = adder(held)
    waiting = [[] for _ in parts]
    for stage in reversed(range(nstages)):
        for q in range(len(parts)):
            if stage == nstages - 1:
                last_add(q)
                spot = (pl.ds(pl.multiple_of(base[q], SUBLANES), size), slice(starts[q], starts[q + 1]))
                total[spot] = prod[spot]
            for copy in waiting[q]:
                copy.wait()
            waiting[q] = share_part(q, stage, slot, size)
            base[q] = marks[q][stage]
        slot += len(waiting[0])
        mat, done = turn_by(mat, done, turns if stage == 0 else 4)
        size <<= len(parts[0][0][stage])

    inverse = -mat
    for q in range(len(parts)):
        for copy in waiting[q]:
            copy.wait()
        first, last = starts[q], starts[q + 1]
        split = min(max(first, cols_dev), last)
        if split > first:
            coefs[:, first:split] = dot_full(inverse, total[:, first:split])
            copy = pltpu.make_async_copy(
                coefs.at[:, pl.ds(first, split - first)], coefs_out.at[:, pl.ds(first, split - first)], out_sem.at[2 + q])
            copy.start()
            keep_copies.append(copy)
        if last > split:
            side[:, split - cols_dev : last - cols_dev] = dot_full(inverse, total[:, split:last])
    copy = pltpu.make_async_copy(side, side_out, out_sem.at[2 + len(parts)])
    copy.start()
    keep_copies.append(copy)
    for copy in keep_copies:
        copy.wait()


def finish(front_hbm, panel_hbm, coefs_hbm, side_hbm, rhs_hbm, updated, side_t, left_t,
           front, panel, coefs, side, rhs_t, stage, in_sem, sems):
    nrhs = rhs_t.shape[0]
    tile = stage.shape[2]
    loads = [
        pltpu.make_async_copy(source, target, in_sem.at[k])
        for k, (source, target) in enumerate(
            [(panel_hbm, panel), (coefs_hbm, coefs), (front_hbm, front), (side_hbm, side), (rhs_hbm, rhs_t)])
    ]
    for load in loads:
        load.start()
    loads[0].wait()
    high, low, _ = pieces(panel[...])
    left = jnp.concatenate([high, high, low], axis=1)

    def product(right):
        top, rest, _ = pieces(right)
        return dot(left, jnp.concatenate([top, rest, top], axis=0), ((1,), (0,)))

    for load in loads[1:]:
        load.wait()
    copies = []
    for t in range(stage.shape[0]):
        at = slice(t * tile, (t + 1) * tile)
        stage[t] = front[:, at] - product(coefs[:, at])
        copy = pltpu.make_async_copy(stage.at[t], updated.at[:, pl.ds(t * tile, tile)], sems.at[t])
        copy.start()
        copies.append(copy)
    sides = side[...]
    side_t[...] = jnp.transpose(sides)[:nrhs]
    left_t[...] = rhs_t[...] - jnp.transpose(product(sides))[:nrhs]
    for copy in copies:
        copy.wait()


def solution(mesh):
    n, ncols = mesh.shape["rows"], mesh.shape["cols"]

    def shards(parent_front, right_sides, child_values, block_owner, row_map, col_map):
        rows_dev, cols_dev = parent_front.shape
        child_rows, child_cols = child_values.shape
        nrhs = right_sides.shape[1]
        side_width = -(-nrhs // LANES) * LANES
        width = cols_dev + side_width
        starts, parts, _ = plan(n, width)
        nparts = len(parts)
        widest = max(starts[q + 1] - starts[q] for q in range(nparts))
        landing_rows, slots = slots_of(n)
        block = child_rows // n
        chunks = min(n, PANEL // SUBLANES)
        vmem = pl.BlockSpec(memory_space=pltpu.VMEM)
        dma = pltpu.SemaphoreType.DMA
        hbm = pl.BlockSpec(memory_space=pltpu.HBM)
        rhs_t = right_sides.T
        front, panel, coefs, side = pl.pallas_call(
            functools.partial(kernel, n, ncols),
            out_shape=(
                jax.ShapeDtypeStruct((rows_dev, cols_dev), f32),
                jax.ShapeDtypeStruct((rows_dev, PANEL), f32),
                jax.ShapeDtypeStruct((PANEL, cols_dev), f32),
                jax.ShapeDtypeStruct((PANEL, side_width), f32),
            ),
            in_specs=[hbm] * 6,
            out_specs=(hbm, hbm, hbm, hbm),
            scratch_shapes=[
                pltpu.VMEM((rows_dev, cols_dev), f32),
                pltpu.VMEM((rows_dev, PANEL), f32),
                pltpu.VMEM((PANEL, cols_dev), f32),
                pltpu.VMEM((PANEL, side_width), f32),
                dma((3 + nparts,)),
                pltpu.SMEM(block_owner.shape, jnp.int32),
                pltpu.VMEM((nrhs, rows_dev), f32),
                pltpu.VMEM((1, child_rows), jnp.int32),
                pltpu.VMEM((1, child_cols), jnp.int32),
                pltpu.VMEM((child_rows, child_cols), f32),
                pltpu.VMEM((n, block, child_cols + LANES), f32),
                pltpu.VMEM((n, block, child_cols + LANES), f32),
                pltpu.VMEM((child_rows, child_cols + LANES), f32),
                pltpu.VMEM((cols_dev, child_cols), bf16),
                pltpu.VMEM((rows_dev, side_width), f32),
                pltpu.VMEM((PANEL, width), f32),
                pltpu.VMEM((PANEL, width), f32),
                pltpu.VMEM((nparts, landing_rows, widest), f32),
                pltpu.VMEM((PANEL, PANEL), f32),
                pltpu.VMEM((n, PANEL // chunks, PANEL), f32),
                pltpu.VMEM((PANEL, PANEL), f32),
                dma((6,)),
                dma((n,)),
                dma((n,)),
                dma((max(ncols - 1, 1),)),
                dma,
                dma((n + chunks,)),
                dma((n + chunks,)),
                dma((nparts, 2 * slots)),
                dma((nparts, 2 * slots)),
            ],
            compiler_params=pltpu.CompilerParams(collective_id=0, has_side_effects=True, vmem_limit_bytes=VMEM_LIMIT),
        )(block_owner, parent_front, rhs_t, child_values, row_map.reshape(1, -1), col_map.reshape(1, -1))
        tile = min(TILE, cols_dev)
        updated, side_t, left_t = pl.pallas_call(
            finish,
            out_shape=(
                jax.ShapeDtypeStruct((rows_dev, cols_dev), f32),
                jax.ShapeDtypeStruct((nrhs, PANEL), f32),
                jax.ShapeDtypeStruct((nrhs, rows_dev), f32),
            ),
            in_specs=[hbm] * 5,
            out_specs=(hbm, vmem, vmem),
            scratch_shapes=[
                pltpu.VMEM((rows_dev, cols_dev), f32),
                pltpu.VMEM((rows_dev, PANEL), f32),
                pltpu.VMEM((PANEL, cols_dev), f32),
                pltpu.VMEM((PANEL, side_width), f32),
                pltpu.VMEM((nrhs, rows_dev), f32),
                pltpu.VMEM((cols_dev // tile, rows_dev, tile), f32),
                dma((5,)),
                dma((cols_dev // tile,)),
            ],
            compiler_params=pltpu.CompilerParams(vmem_limit_bytes=VMEM_LIMIT),
        )(front, panel, coefs, side, rhs_t)
        return updated, side_t.T, left_t.T

    in_specs = (
        P("rows", "cols"),
        P("rows", None),
        P("rows", "cols"),
        P("rows"),
        P("rows"),
        P("cols"),
    )
    out_specs = (P("rows", "cols"), P(), P("rows", None))
    return jax.shard_map(shards, mesh=mesh, in_specs=in_specs, out_specs=out_specs, check_vma=False)
```

profile of v0, /device:TPU:0, one launch (start us, length us, event | category | flops | bytes accessed | tf_op | source)
XLA Modules:
  0.0 44.7 jit_solution(11981633726490267417)
XLA Ops:
  0.6 40.7 %shard_map.85 = (f32[256,1024]{1,0:T(8,128)}, f32[256,128]{1,0:T(8,128)}, f32[128,1024]{1,0:T(8,128)}, f32[128,128]{1,0:T(8,128)}) custom-call(s32[16]{0:T(128)} %owner_hbm.1, f32[256,1024]{1,0:T(8,128)} %parent.1, f32[64,256]{1,0:T(8,128)} %bitcast.5, f32[64,512]{1,0:T(8,128)} %child_hbm.1, s32[1,64]{1,0:T(1,128)} %bitcast.8, s32[1,512]{1,0:T(1,128)} %bitcast.7), custom_call_target="tpu_custom_call" | custom-call | tf_op jit(solution)/shard_map/pallas_call | solution.py:455
  41.3 3.4 %shard_map.86 = (f32[256,1024]{1,0:T(8,128)}, f32[64,128]{1,0:T(8,128)}, f32[64,256]{1,0:T(8,128)}) custom-call(f32[256,1024]{1,0:T(8,128)} %get-tuple-element.10.front_hbm, f32[256,128]{1,0:T(8,128)} %get-tuple-element.11.panel_hbm, f32[128,1024]{1,0:T(8,128)} %get-tuple-element.12.coefs_hbm, f32[128,128]{1,0:T(8,128)} %get-tuple-element.13.side_hbm, ...), custom_call_target="tpu_custom_call" | custom-call | tf_op jit(solution)/shard_map/pallas_call | solution.py:500
where the time goes:
time: 44.9 us; the launch traced here: 44.7 us
  Pallas kernels  44.1 us (98%)
  between operations  0.64 us (1%)
    pallas_call x1, Pallas kernels, shards(): pl.pallas_call(functools.partial(kernel, n, ncols), out_shape=(jax.ShapeD...  40.7 us
    pallas_call x1, Pallas kernels, shards(): pl.pallas_call(finish, out_shape=(jax.ShapeDtypeStruct((rows_dev, cols_de...  3.41 us

commit v1 on v0

--- a/solution.py
+++ b/solution.py
@@ -11,7 +11,7 @@
 LANES = 128
 SUBLANES = 8
 TILE = 256
-VMEM_LIMIT = 67043328
+VMEM_LIMIT = 33521664
 MESH = pl.DeviceIdType.MESH
 f32 = jnp.float32
 bf16 = jnp.bfloat16
@@ -116,7 +116,7 @@
 
 
 def kernel(n, ncols, owner_hbm, parent, rhs_hbm, child_hbm, row_map_hbm, col_map_hbm,
-           front_out, panel_out, coefs_out, side_out, front, panel, coefs, side, out_sem, owner, rhs_t, row_map, col_map, child, send, recv, flat, hot, sides, prod, total, halves, gram, gram_in, gram_all,
+           front, left, inverse, total, panel, owner, rhs_t, row_map, col_map, child, send, recv, flat, hot, sides, prod, halves, gram, gram_in, gram_all,
            in_sem, a2a_send, a2a_recv, pan_send, pan_recv, gram_send, gram_recv, red_send, red_recv):
     row, col = lax.axis_index("rows"), lax.axis_index("cols")
     rows_dev, cols_dev = front.shape
@@ -243,13 +243,6 @@
             prod[:, first:split] = dot_full(block_panel, front[:, first:split], trans)
         if last > split:
             prod[:, split:last] = dot_full(block_panel, sides[:, split - cols_dev : last - cols_dev], trans)
-
-    keep_copies = [
-        pltpu.make_async_copy(front, front_out, out_sem.at[0]),
-        pltpu.make_async_copy(panel, panel_out, out_sem.at[1]),
-    ]
-    for copy in keep_copies:
-        copy.start()
 
     starts, parts, halving = plan(n, prod.shape[1])
     base = [row * 0] * len(parts)
@@ -377,57 +370,33 @@
         mat, done = turn_by(mat, done, turns if stage == 0 else 4)
         size <<= len(parts[0][0][stage])
 
-    inverse = -mat
+    inverse[...] = -mat
+    high, low, _ = pieces(dot_full(block_panel, -mat))
+    left[...] = jnp.concatenate([high, high, low], axis=1)
     for q in range(len(parts)):
         for copy in waiting[q]:
             copy.wait()
-        first, last = starts[q], starts[q + 1]
-        split = min(max(first, cols_dev), last)
-        if split > first:
-            coefs[:, first:split] = dot_full(inverse, total[:, first:split])
-            copy = pltpu.make_async_copy(
-                coefs.at[:, pl.ds(first, split - first)], coefs_out.at[:, pl.ds(first, split - first)], out_sem.at[2 + q])
-            copy.start()
-            keep_copies.append(copy)
-        if last > split:
-            side[:, split - cols_dev : last - cols_dev] = dot_full(inverse, total[:, split:last])
-    copy = pltpu.make_async_copy(side, side_out, out_sem.at[2 + len(parts)])
-    copy.start()
-    keep_copies.append(copy)
-    for copy in keep_copies:
-        copy.wait()
-
-
-def finish(front_hbm, panel_hbm, coefs_hbm, side_hbm, rhs_hbm, updated, side_t, left_t,
-           front, panel, coefs, side, rhs_t, stage, in_sem, sems):
+
+
+def finish(front, left, inverse, total, rhs_t, updated, side_t, left_t, stage, sems):
     nrhs = rhs_t.shape[0]
+    cols_dev = front.shape[1]
     tile = stage.shape[2]
-    loads = [
-        pltpu.make_async_copy(source, target, in_sem.at[k])
-        for k, (source, target) in enumerate(
-            [(panel_hbm, panel), (coefs_hbm, coefs), (front_hbm, front), (side_hbm, side), (rhs_hbm, rhs_t)])
-    ]
-    for load in loads:
-        load.start()
-    loads[0].wait()
-    high, low, _ = pieces(panel[...])
-    left = jnp.concatenate([high, high, low], axis=1)
+    left = left[...]
 
     def product(right):
         top, rest, _ = pieces(right)
         return dot(left, jnp.concatenate([top, rest, top], axis=0), ((1,), (0,)))
 
-    for load in loads[1:]:
-        load.wait()
     copies = []
     for t in range(stage.shape[0]):
         at = slice(t * tile, (t + 1) * tile)
-        stage[t] = front[:, at] - product(coefs[:, at])
+        stage[t] = front[:, at] - product(total[:, at])
         copy = pltpu.make_async_copy(stage.at[t], updated.at[:, pl.ds(t * tile, tile)], sems.at[t])
         copy.start()
         copies.append(copy)
-    sides = side[...]
-    side_t[...] = jnp.transpose(sides)[:nrhs]
+    sides = total[:, cols_dev:]
+    side_t[...] = jnp.transpose(dot_full(inverse[...], sides))[:nrhs]
     left_t[...] = rhs_t[...] - jnp.transpose(product(sides))[:nrhs]
     for copy in copies:
         copy.wait()
@@ -452,22 +421,19 @@
         dma = pltpu.SemaphoreType.DMA
         hbm = pl.BlockSpec(memory_space=pltpu.HBM)
         rhs_t = right_sides.T
-        front, panel, coefs, side = pl.pallas_call(
+        operands = (block_owner, parent_front, rhs_t, child_values, row_map.reshape(1, -1), col_map.reshape(1, -1))
+        front, left, inverse, total = pl.pallas_call(
             functools.partial(kernel, n, ncols),
             out_shape=(
-                jax.ShapeDtypeStruct((rows_dev, cols_dev), f32),
-                jax.ShapeDtypeStruct((rows_dev, PANEL), f32),
-                jax.ShapeDtypeStruct((PANEL, cols_dev), f32),
-                jax.ShapeDtypeStruct((PANEL, side_width), f32),
+                pltpu.VMEM((rows_dev, cols_dev), f32),
+                pltpu.VMEM((rows_dev, 3 * PANEL), bf16),
+                pltpu.VMEM((PANEL, PANEL), f32),
+                pltpu.VMEM((PANEL, width), f32),
             ),
             in_specs=[hbm] * 6,
-            out_specs=(hbm, hbm, hbm, hbm),
+            out_specs=(vmem, vmem, vmem, vmem),
             scratch_shapes=[
-                pltpu.VMEM((rows_dev, cols_dev), f32),
                 pltpu.VMEM((rows_dev, PANEL), f32),
-                pltpu.VMEM((PANEL, cols_dev), f32),
-                pltpu.VMEM((PANEL, side_width), f32),
-                dma((3 + nparts,)),
                 pltpu.SMEM(block_owner.shape, jnp.int32),
                 pltpu.VMEM((nrhs, rows_dev), f32),
                 pltpu.VMEM((1, child_rows), jnp.int32),
@@ -478,7 +444,6 @@
                 pltpu.VMEM((child_rows, child_cols + LANES), f32),
                 pltpu.VMEM((cols_dev, child_cols), bf16),
                 pltpu.VMEM((rows_dev, side_width), f32),
-                pltpu.VMEM((PANEL, width), f32),
                 pltpu.VMEM((PANEL, width), f32),
                 pltpu.VMEM((nparts, landing_rows, widest), f32),
                 pltpu.VMEM((PANEL, PANEL), f32),
@@ -495,7 +460,7 @@
                 dma((nparts, 2 * slots)),
             ],
             compiler_params=pltpu.CompilerParams(collective_id=0, has_side_effects=True, vmem_limit_bytes=VMEM_LIMIT),
-        )(block_owner, parent_front, rhs_t, child_values, row_map.reshape(1, -1), col_map.reshape(1, -1))
+        )(*[pltpu.with_memory_space_constraint(value, pltpu.HBM) for value in operands])
         tile = min(TILE, cols_dev)
         updated, side_t, left_t = pl.pallas_call(
             finish,
@@ -504,20 +469,14 @@
                 jax.ShapeDtypeStruct((nrhs, PANEL), f32),
                 jax.ShapeDtypeStruct((nrhs, rows_dev), f32),
             ),
-            in_specs=[hbm] * 5,
+            in_specs=[vmem] * 5,
             out_specs=(hbm, vmem, vmem),
             scratch_shapes=[
-                pltpu.VMEM((rows_dev, cols_dev), f32),
-                pltpu.VMEM((rows_dev, PANEL), f32),
-                pltpu.VMEM((PANEL, cols_dev), f32),
-                pltpu.VMEM((PANEL, side_width), f32),
-                pltpu.VMEM((nrhs, rows_dev), f32),
                 pltpu.VMEM((cols_dev // tile, rows_dev, tile), f32),
-                dma((5,)),
                 dma((cols_dev // tile,)),
             ],
             compiler_params=pltpu.CompilerParams(vmem_limit_bytes=VMEM_LIMIT),
-        )(front, panel, coefs, side, rhs_t)
+        )(front, left, inverse, total, rhs_t)
         return updated, side_t.T, left_t.T
 
     in_specs = (

time: 44.9 us -> 42.4 us (0.944)
  Pallas kernels: 44.1 us -> 41.6 us
    pallas_call x1, Pallas kernels: 3.41 us -> 1.94 us  [shards(): pl.pallas_call(finish, out_shape=(jax.ShapeDtypeStruct((rows_dev, cols_de...]
    pallas_call x1, Pallas kernels: 40.7 us -> 39.6 us  [shards(): pl.pallas_call(functools.partial(kernel, n, ncols), out_shape=(pltpu.VMEM...]
where the time goes in v1:
time: 42.4 us; the launch traced here: 42.2 us
  Pallas kernels  41.6 us (98%)
  between operations  0.66 us (2%)
    pallas_call x1, Pallas kernels, shards(): pl.pallas_call(functools.partial(kernel, n, ncols), out_shape=(pltpu.VMEM...  39.6 us
    pallas_call x1, Pallas kernels, shards(): pl.pallas_call(finish, out_shape=(jax.ShapeDtypeStruct((rows_dev, cols_de...  1.94 us

profile of v1, /device:TPU:0, one launch (start us, length us, event | category | flops | bytes accessed | tf_op | source)
XLA Modules:
  0.0 42.2 jit_solution(5862028192454375837)
XLA Ops:
  0.6 0.0 copy-start
  0.6 39.6 %shard_map.85 = (f32[256,1024]{1,0:T(8,128)S(1)}, bf16[256,384]{1,0:T(8,128)(2,1)S(1)}, f32[128,128]{1,0:T(8,128)S(1)}, f32[128,1152]{1,0:T(8,128)S(1)}) custom-call(s32[16]{0:T(128)} %owner_hbm.1, f32[256,1024]{1,0:T(8,128)} %parent.1, f32[64,256]{1,0:T(8,128)} %bitcast.5, f32[64,512]{1,0:T(8,128)} %child_hbm.1, s32[1,64]{1,0:T(1,128)} %bitcast.8, ...), custom_call_target="tpu_custom_call" | custom-call | tf_op jit(solution)/shard_map/pallas_call | solution.py:425
  40.3 0.0 copy-done
  40.3 1.9 %shard_map.86 = (f32[256,1024]{1,0:T(8,128)}, f32[64,128]{1,0:T(8,128)}, f32[64,256]{1,0:T(8,128)}) custom-call(f32[256,1024]{1,0:T(8,128)S(1)} %get-tuple-element.10.front, bf16[256,384]{1,0:T(8,128)(2,1)S(1)} %get-tuple-element.11.left, f32[128,128]{1,0:T(8,128)S(1)} %get-tuple-element.12.inverse, f32[128,1152]{1,0:T(8,128)S(1)} %get-tuple-element.13.total, ...), custom_call_target="tpu_custom_call" | custom-call | tf_op jit(solution)/shard_map/pallas_call | solution.py:465
Async XLA Ops:
  0.6 39.6 %copy-start = (f32[256,64]{0,1:T(8,128)S(1)}, f32[256,64]{0,1:T(8,128)}, u32[]{:S(2)}) copy-start(f32[256,64]{0,1:T(8,128)} %param.7) | copy-start | bytes 196612

commit v2 on v1

v2 whole, which is shorter than its diff:
```python
import functools

import jax
import jax.numpy as jnp
from jax import lax
from jax.experimental import pallas as pl
from jax.experimental.pallas import tpu as pltpu
from jax.sharding import PartitionSpec as P

PANEL = 128
LANES = 128
SUBLANES = 8
TILE = 256
NPARTS = 3
SHARES = (6, 6, 4)
VMEM_LIMIT = 33521664
MESH = pl.DeviceIdType.MESH
f32 = jnp.float32
bf16 = jnp.bfloat16


def pieces(value):
    first = value.astype(bf16)
    rest = value - first.astype(f32)
    second = rest.astype(bf16)
    third = (rest - second.astype(f32)).astype(bf16)
    return first, second, third


def dot(left, right, dims, precision=None):
    return lax.dot_general(left, right, (dims, ((), ())), precision=precision, preferred_element_type=f32)


def dot_full(left, right, dims=((1,), (0,))):
    return dot(left, right, dims, lax.Precision.HIGHEST)


def inverse_pair(a, b, d):
    ia = 1.0 / a
    ratio = b * ia
    i11 = 1.0 / (d - b * ratio)
    i01 = -ratio * i11
    return ia - ratio * i01, i01, i11


def sweep_four(mat, k, lane):
    cols = [mat[:, k + j : k + j + 1] for j in range(4)]
    rows = [mat[k + j : k + j + 1, :] for j in range(4)]
    d = [[jnp.broadcast_to(mat[k + i : k + i + 1, k + j : k + j + 1], (1, mat.shape[1])) for j in range(i + 1)] for i in range(4)]
    a00, a01, a11 = inverse_pair(d[0][0], d[1][0], d[1][1])
    l20, l21 = d[2][0] * a00 + d[2][1] * a01, d[2][0] * a01 + d[2][1] * a11
    l30, l31 = d[3][0] * a00 + d[3][1] * a01, d[3][0] * a01 + d[3][1] * a11
    s22 = d[2][2] - (l20 * d[2][0] + l21 * d[2][1])
    s32 = d[3][2] - (l30 * d[2][0] + l31 * d[2][1])
    s33 = d[3][3] - (l30 * d[3][0] + l31 * d[3][1])
    e22, e32, e33 = inverse_pair(s22, s32, s33)
    e20, e21 = -(e22 * l20 + e32 * l30), -(e22 * l21 + e32 * l31)
    e30, e31 = -(e32 * l20 + e33 * l30), -(e32 * l21 + e33 * l31)
    e00 = a00 - (l20 * e20 + l30 * e30)
    e10 = a01 - (l21 * e20 + l31 * e30)
    e11 = a11 - (l21 * e21 + l31 * e31)
    e = [[e00, e10, e20, e30], [e10, e11, e21, e31], [e20, e21, e22, e32], [e30, e31, e32, e33]]
    lane_row = lane[:1]
    tops = []
    for i in range(4):
        top = (e[i][0] * rows[0] + e[i][1] * rows[1]) + (e[i][2] * rows[2] + e[i][3] * rows[3])
        for j in range(4):
            top = jnp.where(lane_row == k + j, -e[i][j], top)
        tops.append(top)
    out = jnp.where((lane >= k) & (lane < k + 4), 0.0, mat)
    out = out - ((cols[0] * tops[0] + cols[1] * tops[1]) + (cols[2] * tops[2] + cols[3] * tops[3]))
    head = out[:SUBLANES]
    sub = lax.broadcasted_iota(jnp.int32, head.shape, 0)
    for j in range(4):
        head = jnp.where(sub == k + j, tops[j], head)
    return jnp.concatenate([head, out[SUBLANES:]], axis=0)


def sweep_groups(mat, count):
    size = mat.shape[0]
    lane = lax.broadcasted_iota(jnp.int32, mat.shape, 1)

    def group(_, mat):
        for k in range(0, SUBLANES, 4):
            mat = sweep_four(mat, k, lane)
        mat = jnp.concatenate([mat[SUBLANES:], mat[:SUBLANES]], axis=0)
        return pltpu.roll(mat, size - SUBLANES, 1)

    return lax.fori_loop(0, count, group, mat)


def flipped(index, code):
    for bit in range(code.bit_length()):
        if code >> bit & 1:
            index = index + (1 - 2 * ((index // (1 << bit)) % 2)) * (1 << bit)
    return index


def plan(n, width):
    levels = n.bit_length() - 1
    halving = min(levels, (PANEL // SUBLANES).bit_length() - 1)
    norders = min(3, levels)
    tiles = width // LANES
    nparts = min(NPARTS, tiles)
    sizes = [tiles // nparts + (q < tiles % nparts) for q in range(nparts)]
    starts = [LANES * sum(sizes[:q]) for q in range(nparts + 1)]
    orders = [[(q + t) % norders for t in range(norders)] + list(range(norders, levels)) for q in range(nparts)]
    single = max(halving - 2, 0)
    cuts = [(t, t + 1) for t in range(single)] + [(single, halving)]
    parts = [([order[a:b] for a, b in cuts], [[bit] for bit in order[halving:]]) for order in orders]
    return starts, parts, halving


def landing_of(n):
    levels = n.bit_length() - 1
    halving = min(levels, (PANEL // SUBLANES).bit_length() - 1)
    single = max(halving - 2, 0)
    rows, size = 0, PANEL
    for bits in [1] * single + [halving - single]:
        size >>= bits
        rows += ((1 << bits) - 1) * size
    return rows + (levels - halving) * SUBLANES, single + 1, levels - halving


def landed(ref, send_sem, recv_sem, peer):
    return pltpu.make_async_remote_copy(
        src_ref=ref, dst_ref=ref, send_sem=send_sem, recv_sem=recv_sem, device_id=peer, device_id_type=MESH)


def kernel(n, ncols, owner_hbm, parent, rhs_hbm, child_hbm, row_map_hbm, col_map_hbm,
           front, left, inverse, total, side, panel, owner, rhs_t, row_map, col_map, child,
           lead_out, lead_in, tail_out, tail_in, flat, hot, prod, halves, gram, gram_in, gram_all,
           in_sem, lead_sem, tail_sem, pan_sem, gram_sem, side_sem, send_sem, recv_sem, extra_sem):
    row, col = lax.axis_index("rows"), lax.axis_index("cols")
    rows_dev, cols_dev = front.shape
    child_rows, child_cols = child.shape
    nrhs = rhs_t.shape[0]
    block = child_rows // n
    spare = cols_dev - child_cols
    other = (flipped(row, 1), col)
    first_loads = [
        pltpu.make_async_copy(source, target, in_sem.at[k])
        for k, (source, target) in enumerate([(owner_hbm, owner), (row_map_hbm, row_map), (child_hbm, child)])
    ]
    later_loads = [
        pltpu.make_async_copy(source, target, in_sem.at[3 + k])
        for k, (source, target) in enumerate([(col_map_hbm, col_map), (rhs_hbm, rhs_t), (parent, front)])
    ]
    for load in first_loads + later_loads:
        load.start()

    barrier = pltpu.get_barrier_semaphore()
    for code in reversed(range(1, n)):
        pl.semaphore_signal(barrier, inc=1, device_id=(flipped(row, code), col), device_id_type=MESH)
    for step in range(1, ncols):
        pl.semaphore_signal(barrier, inc=1, device_id=(row, lax.rem(col + step, ncols)), device_id_type=MESH)

    for load in first_loads:
        load.wait()
    source = lax.broadcasted_iota(jnp.int32, (1, child_rows), 1)
    target = jnp.zeros((1, child_rows), jnp.int32)
    for k in range(n):
        target = jnp.where(source // block == k, owner[k] * block + source % block, target)
    place = lax.broadcasted_iota(jnp.int32, (child_rows, child_rows), 0) == target
    place_f = jnp.where(place, 1.0, 0.0).astype(f32)
    landing = jnp.sum(place_f * row_map[...].astype(f32), axis=1, keepdims=True)
    place_b = place_f.astype(bf16)
    one, two, three = pieces(child[...])
    ordered = dot(place_b, one, ((1,), (0,))) + dot(place_b, two, ((1,), (0,))) + dot(place_b, three, ((1,), (0,)))
    slot_of = lax.broadcasted_iota(jnp.int32, (child_rows, LANES), 0)
    lane_of = lax.broadcasted_iota(jnp.int32, (child_rows, LANES), 1)
    spots = jnp.where(lane_of == row * block + slot_of % block, landing, 0.0)
    pick = lax.broadcasted_iota(jnp.int32, (n, child_rows), 0) == lax.broadcasted_iota(jnp.int32, (n, child_rows), 1) // block
    heads = dot_full(jnp.where(pick, 1.0, 0.0).astype(f32), spots)
    for k in range(n):
        lead_out[k, :block] = ordered[k * block : (k + 1) * block, :LANES]
        lead_out[k, block : block + 1] = heads[k : k + 1]
        tail_out[k] = ordered[k * block : (k + 1) * block, LANES:]

    pl.semaphore_wait(barrier, n - 1 + ncols - 1)

    for source_ref, target_ref, sem in ((lead_out, lead_in, lead_sem), (tail_out, tail_in, tail_sem)):
        for code in reversed(range(1, n)):
            peer = flipped(row, code)
            pltpu.make_async_remote_copy(
                src_ref=source_ref.at[peer], dst_ref=target_ref.at[row], send_sem=sem.at[0], recv_sem=sem.at[1],
                device_id=(peer, col), device_id_type=MESH).start()
    lead_in[row] = lead_out[row]
    tail_in[row] = tail_out[row]

    for load in later_loads:
        load.wait()
    cols_at = lax.broadcasted_iota(jnp.int32, hot.shape, 0)
    hot[...] = jnp.where(cols_at == col_map[...], 1.0, 0.0).astype(f32).astype(bf16)
    padded = jnp.concatenate([rhs_t[...], jnp.zeros((LANES - nrhs, rows_dev), f32)], axis=0)
    sides = jnp.transpose(padded)

    lead_all = landed(lead_in.at[pl.ds(0, n - 1)], lead_sem.at[0], lead_sem.at[1], other)
    lead_all.wait_recv()
    heads = lead_in[0, block : block + 1]
    for k in range(1, n):
        heads = heads + lead_in[k, block : block + 1]
    for k in range(n):
        flat[k * block : (k + 1) * block, :LANES] = lead_in[k, :block]
    spot = lax.broadcasted_iota(jnp.int32, (rows_dev, child_rows), 0) == heads[:, :child_rows].astype(jnp.int32)
    spot_b = jnp.where(spot, 1.0, 0.0).astype(f32).astype(bf16)
    spot3 = jnp.concatenate([spot_b] * 3, axis=1)

    def assemble(vals, first, last):
        low = max(0, first - spare) // LANES * LANES
        high = min(child_cols, last)
        spread = dot(vals[:, low:high], hot[first:last, low:high], ((1,), (1,)))
        front[:, first:last] = front[:, first:last] + dot(spot3, spread.astype(bf16), ((1,), (0,)))

    lead_vals = jnp.concatenate(pieces(flat[:, :LANES]), axis=0)
    assemble(lead_vals, 0, PANEL)
    pan_copies = [
        pltpu.make_async_remote_copy(
            src_ref=front.at[:, pl.ds(0, PANEL)], dst_ref=panel, send_sem=pan_sem.at[1 + step], recv_sem=pan_sem.at[0],
            device_id=(row, step), device_id_type=MESH)
        for step in range(1, ncols)
    ]

    @pl.when(col == 0)
    def _():
        for copy in pan_copies:
            copy.start()
        panel[...] = front[:, :PANEL]

    @pl.when(col != 0)
    def _():
        pan_copies[0].wait_recv()

    block_panel = panel[...]
    turned = jnp.transpose(block_panel)
    gram[...] = dot_full(turned, block_panel)

    chunks = min(n, PANEL // SUBLANES)
    chunk = PANEL // chunks
    own_chunk = lax.rem(row, chunks)
    own_rows = pl.ds(pl.multiple_of(own_chunk * chunk, SUBLANES), chunk)
    for code in reversed(range(1, n)):
        peer = flipped(row, code)
        start = pl.multiple_of(lax.rem(peer, chunks) * chunk, SUBLANES)
        pltpu.make_async_remote_copy(
            src_ref=gram.at[pl.ds(start, chunk)], dst_ref=gram_in.at[row],
            send_sem=gram_sem.at[0], recv_sem=gram_sem.at[1], device_id=(peer, col), device_id_type=MESH).start()
    gram_in[row] = gram[own_rows, :]

    tail_all = landed(tail_in.at[pl.ds(0, n - 1)], tail_sem.at[0], tail_sem.at[1], other)
    tail_all.wait_recv()
    for k in range(n):
        flat[k * block : (k + 1) * block, LANES:] = tail_in[k]
    vals = jnp.concatenate([lead_vals, jnp.concatenate(pieces(flat[:, LANES:]), axis=0)], axis=1)
    first = PANEL
    while first < cols_dev:
        last = min(cols_dev, (first // TILE + 1) * TILE)
        assemble(vals, first, last)
        first = last

    high, low, _ = pieces(turned)
    turned3 = jnp.concatenate([high, high, low], axis=1)
    opening = jnp.where(col == 0, sides, front[:, :PANEL])

    def products(first, last):
        def product(right):
            top, rest, _ = pieces(right)
            return dot(turned3, jnp.concatenate([top, rest, top], axis=0), ((1,), (0,)))

        if first == 0:
            prod[:, :PANEL] = product(opening)
            first = PANEL
        if last > first:
            prod[:, first:last] = product(front[:, first:last])

    starts, parts, halving = plan(n, prod.shape[1])
    base = [row * 0] * len(parts)
    nstages = len(parts[0][0])

    def own_bit(bit):
        return (row // (1 << bit)) % 2

    def members(bits):
        mine = sum(own_bit(bit) * (1 << i) for i, bit in enumerate(bits))
        others = []
        for d in reversed(range(1, 1 << len(bits))):
            code, peer = 0, row
            for i, bit in enumerate(bits):
                own = own_bit(bit)
                flip = d >> i & 1
                code = code + (1 - own if flip else own) * (1 << i)
                peer = peer + ((1 - 2 * own) * (1 << bit) if flip else 0)
            others.append((code, peer))
        return mine, others

    def send_part(q, stage, at, size, split):
        groups, extras = parts[q]
        bits = groups[stage] if split else extras[stage]
        mine, others = members(bits)
        piece = size >> len(bits) if split else size
        keep = pl.multiple_of(base[q] + mine * piece if split else base[q], SUBLANES)
        width = starts[q + 1] - starts[q]
        send, recv = (send_sem.at[0], recv_sem.at[q, stage]) if split else (extra_sem.at[0, q, stage], extra_sem.at[1, q, stage])
        for d, (code, peer) in enumerate(others):
            give = pl.multiple_of(base[q] + code * piece, SUBLANES) if split else keep
            pltpu.make_async_remote_copy(
                src_ref=prod.at[pl.ds(give, piece), pl.ds(starts[q], width)],
                dst_ref=halves.at[q, pl.ds(at + d * piece, piece), pl.ds(0, width)],
                send_sem=send, recv_sem=recv, device_id=(peer, col), device_id_type=MESH).start()
        base[q] = keep
        return len(others), at, send, recv, keep, piece, width

    def send_stage(stage, at, size, split, before):
        held = []
        for q in range(len(parts)):
            before(q)
            if split:
                marks[q].append(base[q])
            held.append(send_part(q, stage, at, size, split))
        used, piece = held[0][0], held[0][5]
        return (held, split), at + used * piece, piece

    def adder(state):
        held, split = state

        def add_part(q):
            used, at, send, recv, keep, piece, width = held[q]
            whole = landed(halves.at[q, pl.ds(at, used * piece), pl.ds(0, width)], send, recv, other)
            whole.wait_recv()
            if not split:
                whole.wait_send()
            spot = (pl.ds(keep, piece), slice(starts[q], starts[q + 1]))
            value = prod[spot]
            for d in range(used):
                value = value + halves[q, at + d * piece : at + (d + 1) * piece, :width]
            prod[spot] = value

        return add_part

    def share_part(q, stage, piece):
        _, others = members(parts[q][0][stage])
        keep = pl.multiple_of(base[q], SUBLANES)
        columns = pl.ds(starts[q], starts[q + 1] - starts[q])
        spot = total.at[pl.ds(keep, piece), columns]
        recv = recv_sem.at[q, nstages + stage]
        for _, peer in others:
            pltpu.make_async_remote_copy(
                src_ref=spot, dst_ref=spot, send_sem=send_sem.at[1], recv_sem=recv,
                device_id=(peer, col), device_id_type=MESH).start()
        return landed(total.at[pl.ds(0, len(others) * piece), columns], send_sem.at[1], recv, other)

    marks = [[] for _ in parts]
    at, size = 0, PANEL
    held, at, size = send_stage(0, at, size, True, lambda q: products(starts[q], starts[q + 1]))

    gathered = landed(gram_in.at[pl.ds(0, n - 1)], gram_sem.at[0], gram_sem.at[1], other)
    gathered.wait_recv()
    summed = gram_in[0]
    for k in range(1, n):
        summed = summed + gram_in[k]
    gram_all[own_rows, :] = summed
    for code in reversed(range(1, chunks)):
        peer = row - own_chunk + flipped(own_chunk, code)
        pltpu.make_async_remote_copy(
            src_ref=gram_all.at[own_rows], dst_ref=gram_all.at[own_rows],
            send_sem=gram_sem.at[2], recv_sem=gram_sem.at[3], device_id=(peer, col), device_id_type=MESH).start()

    for stage in range(1, nstages):
        held, at, size = send_stage(stage, at, size, True, adder(held))
    spread_all = landed(gram_all.at[pl.ds(0, (chunks - 1) * chunk)], gram_sem.at[2], gram_sem.at[3], other)
    spread_all.wait_recv()
    turns = PANEL // SUBLANES
    mat, done = gram_all[...], 0

    def turn_by(mat, done, share):
        upto = min(turns, done + share)
        return (sweep_groups(mat, upto - done) if upto > done else mat), upto

    mat, done = turn_by(mat, done, SHARES[0])
    for stage in range(len(parts[0][1])):
        held, at, size = send_stage(stage, at, size, False, adder(held))
    last_add = adder(held)
    waiting = [None for _ in parts]
    for stage in reversed(range(nstages)):
        for q in range(len(parts)):
            if stage == nstages - 1:
                last_add(q)
                spot = (pl.ds(pl.multiple_of(base[q], SUBLANES), size), slice(starts[q], starts[q + 1]))
                total[spot] = prod[spot]
            else:
                waiting[q].wait_recv()
            waiting[q] = share_part(q, stage, size)
            base[q] = marks[q][stage]
        mat, done = turn_by(mat, done, turns if stage == 0 else SHARES[1 + nstages - 1 - stage])
        size <<= len(parts[0][0][stage])

    inverse[...] = -mat
    high, low, _ = pieces(dot_full(block_panel, -mat))
    left[...] = jnp.concatenate([high, high, low], axis=1)
    for q in range(len(parts)):
        waiting[q].wait_recv()
        if q == 0:
            side_copies = [
                pltpu.make_async_remote_copy(
                    src_ref=side, dst_ref=side, send_sem=side_sem.at[1 + step], recv_sem=side_sem.at[0],
                    device_id=(row, step), device_id_type=MESH)
                for step in range(1, ncols)
            ]

            @pl.when(col == 0)
            def _():
                side[...] = total[:, :PANEL]
                for copy in side_copies:
                    copy.start()

    lead_all.wait_send()
    tail_all.wait_send()
    gathered.wait_send()
    spread_all.wait_send()
    for k in range(2):
        landed(total.at[pl.ds(0, PANEL - (PANEL >> halving))], send_sem.at[k], send_sem.at[k], other).wait_send()

    @pl.when(col == 0)
    def _():
        for copy in pan_copies + side_copies:
            copy.wait_send()
        total[:, :PANEL] = gram_all[...]

    @pl.when(col != 0)
    def _():
        side_copies[0].wait_recv()


def finish(front, left, inverse, total, side, rhs_t, updated, side_t, left_t, stage, sems):
    nrhs = rhs_t.shape[0]
    tile = stage.shape[2]
    left = left[...]

    def product(right):
        top, rest, _ = pieces(right)
        return dot(left, jnp.concatenate([top, rest, top], axis=0), ((1,), (0,)))

    copies = []
    for t in range(stage.shape[0]):
        at = slice(t * tile, (t + 1) * tile)
        stage[t] = front[:, at] - product(total[:, at])
        copy = pltpu.make_async_copy(stage.at[t], updated.at[:, pl.ds(t * tile, tile)], sems.at[t])
        copy.start()
        copies.append(copy)
    sides = side[...]
    side_t[...] = jnp.transpose(dot_full(inverse[...], sides))[:nrhs]
    left_t[...] = rhs_t[...] - jnp.transpose(product(sides))[:nrhs]
    for copy in copies:
        copy.wait()


def solution(mesh):
    n, ncols = mesh.shape["rows"], mesh.shape["cols"]

    def shards(parent_front, right_sides, child_values, block_owner, row_map, col_map):
        rows_dev, cols_dev = parent_front.shape
        child_rows, child_cols = child_values.shape
        nrhs = right_sides.shape[1]
        starts, parts, _ = plan(n, cols_dev)
        nparts = len(parts)
        widest = max(starts[q + 1] - starts[q] for q in range(nparts))
        landing_rows, nstages, nextra = landing_of(n)
        block = child_rows // n
        chunks = min(n, PANEL // SUBLANES)
        vmem = pl.BlockSpec(memory_space=pltpu.VMEM)
        dma = pltpu.SemaphoreType.DMA
        hbm = pl.BlockSpec(memory_space=pltpu.HBM)
        rhs_t = right_sides.T
        operands = (block_owner, parent_front, rhs_t, child_values, row_map.reshape(1, -1), col_map.reshape(1, -1))
        front, left, inverse, total, side = pl.pallas_call(
            functools.partial(kernel, n, ncols),
            out_shape=(
                pltpu.VMEM((rows_dev, cols_dev), f32),
                pltpu.VMEM((rows_dev, 3 * PANEL), bf16),
                pltpu.VMEM((PANEL, PANEL), f32),
                pltpu.VMEM((PANEL, cols_dev), f32),
                pltpu.VMEM((PANEL, LANES), f32),
            ),
            in_specs=[hbm] * 6,
            out_specs=(vmem,) * 5,
            scratch_shapes=[
                pltpu.VMEM((rows_dev, PANEL), f32),
                pltpu.SMEM(block_owner.shape, jnp.int32),
                pltpu.VMEM((nrhs, rows_dev), f32),
                pltpu.VMEM((1, child_rows), jnp.int32),
                pltpu.VMEM((1, child_cols), jnp.int32),
                pltpu.VMEM((child_rows, child_cols), f32),
                pltpu.VMEM((n, block + 1, LANES), f32),
                pltpu.VMEM((n, block + 1, LANES), f32),
                pltpu.VMEM((n, block, child_cols - LANES), f32),
                pltpu.VMEM((n, block, child_cols - LANES), f32),
                pltpu.VMEM((child_rows, child_cols), f32),
                pltpu.VMEM((cols_dev, child_cols), bf16),
                pltpu.VMEM((PANEL, cols_dev), f32),
                pltpu.VMEM((nparts, landing_rows, widest), f32),
                pltpu.VMEM((PANEL, PANEL), f32),
                pltpu.VMEM((n, PANEL // chunks, PANEL), f32),
                pltpu.VMEM((PANEL, PANEL), f32),
                dma((6,)),
                dma((2,)),
                dma((2,)),
                dma((ncols + 1,)),
                dma((4,)),
                dma((ncols + 1,)),
                dma((2,)),
                dma((nparts, 2 * nstages)),
                dma((2, nparts, max(nextra, 1))),
            ],
            compiler_params=pltpu.CompilerParams(collective_id=0, has_side_effects=True, vmem_limit_bytes=VMEM_LIMIT),
        )(*[pltpu.with_memory_space_constraint(value, pltpu.HBM) for value in operands])
        tile = min(TILE, cols_dev)
        updated, side_t, left_t = pl.pallas_call(
            finish,
            out_shape=(
                jax.ShapeDtypeStruct((rows_dev, cols_dev), f32),
                jax.ShapeDtypeStruct((nrhs, PANEL), f32),
                jax.ShapeDtypeStruct((nrhs, rows_dev), f32),
            ),
            in_specs=[vmem] * 6,
            out_specs=(hbm, vmem, vmem),
            scratch_shapes=[
                pltpu.VMEM((cols_dev // tile, rows_dev, tile), f32),
                dma((cols_dev // tile,)),
            ],
            compiler_params=pltpu.CompilerParams(vmem_limit_bytes=VMEM_LIMIT),
        )(front, left, inverse, total, side, rhs_t)
        return updated, side_t.T, left_t.T

    in_specs = (
        P("rows", "cols"),
        P("rows", None),
        P("rows", "cols"),
        P("rows"),
        P("rows"),
        P("cols"),
    )
    out_specs = (P("rows", "cols"), P(), P("rows", None))
    return jax.shard_map(shards, mesh=mesh, in_specs=in_specs, out_specs=out_specs, check_vma=False)
```

time: 42.4 us -> 39.9 us (0.941)
  Pallas kernels: 41.6 us -> 39.1 us
    pallas_call x1, Pallas kernels: 39.6 us -> 37.2 us  [shards(): pl.pallas_call(functools.partial(kernel, n, ncols), out_shape=(pltpu.VMEM...]
where the time goes in v2:
time: 39.9 us; the launch traced here: 39.8 us
  Pallas kernels  39.1 us (98%)
  between operations  0.66 us (2%)
    pallas_call x1, Pallas kernels, shards(): pl.pallas_call(functools.partial(kernel, n, ncols), out_shape=(pltpu.VMEM...  37.2 us
    pallas_call x1, Pallas kernels, shards(): pl.pallas_call(finish, out_shape=(jax.ShapeDtypeStruct((rows_dev, cols_de...  1.94 us

profile of v2, /device:TPU:0, one launch (start us, length us, event | category | flops | bytes accessed | tf_op | source)
XLA Modules:
  0.0 39.8 jit_solution(311770187750383560)
XLA Ops:
  0.6 0.0 copy-start
  0.6 37.2 %shard_map.85 = (f32[256,1024]{1,0:T(8,128)S(1)}, bf16[256,384]{1,0:T(8,128)(2,1)S(1)}, f32[128,128]{1,0:T(8,128)S(1)}, f32[128,1024]{1,0:T(8,128)S(1)}, f32[128,128]{1,0:T(8,128)S(1)}) custom-call(s32[16]{0:T(128)} %owner_hbm.1, f32[256,1024]{1,0:T(8,128)} %parent.1, f32[64,256]{1,0:T(8,128)} %bitcast.5, f32[64,512]{1,0:T(8,128)} %child_hbm.1, ...), custom_call_target="tpu_custom_call" | custom-call | tf_op jit(solution)/shard_map/pallas_call | solution.py:475
  37.8 0.0 copy-done
  37.9 1.9 %shard_map.86 = (f32[256,1024]{1,0:T(8,128)}, f32[64,128]{1,0:T(8,128)}, f32[64,256]{1,0:T(8,128)}) custom-call(f32[256,1024]{1,0:T(8,128)S(1)} %get-tuple-element.11.front, bf16[256,384]{1,0:T(8,128)(2,1)S(1)} %get-tuple-element.12.left, f32[128,128]{1,0:T(8,128)S(1)} %get-tuple-element.13.inverse, f32[128,1024]{1,0:T(8,128)S(1)} %get-tuple-element.14.total, ...), custom_call_target="tpu_custom_call" | custom-call | tf_op jit(solution)/shard_map/pallas_call | solution.py:517
Async XLA Ops:
  0.6 37.2 %copy-start = (f32[256,64]{0,1:T(8,128)S(1)}, f32[256,64]{0,1:T(8,128)}, u32[]{:S(2)}) copy-start(f32[256,64]{0,1:T(8,128)} %param.7) | copy-start | bytes 196612

commit v3 on v2

--- a/solution.py
+++ b/solution.py
@@ -11,7 +11,7 @@
 LANES = 128
 SUBLANES = 8
 TILE = 256
-NPARTS = 3
+NPARTS = 6
 SHARES = (6, 6, 4)
 VMEM_LIMIT = 33521664
 MESH = pl.DeviceIdType.MESH
@@ -129,7 +129,7 @@
 
 def kernel(n, ncols, owner_hbm, parent, rhs_hbm, child_hbm, row_map_hbm, col_map_hbm,
            front, left, inverse, total, side, panel, owner, rhs_t, row_map, col_map, child,
-           lead_out, lead_in, tail_out, tail_in, flat, hot, prod, halves, gram, gram_in, gram_all,
+           lead_out, lead_in, tail_out, tail_in, flat, stacked, spread_at, turned3, hot, prod, halves, gram, gram_in, gram_all,
            in_sem, lead_sem, tail_sem, pan_sem, gram_sem, side_sem, send_sem, recv_sem, extra_sem):
     row, col = lax.axis_index("rows"), lax.axis_index("cols")
     rows_dev, cols_dev = front.shape
@@ -204,13 +204,13 @@
         flat[k * block : (k + 1) * block, :LANES] = lead_in[k, :block]
     spot = lax.broadcasted_iota(jnp.int32, (rows_dev, child_rows), 0) == heads[:, :child_rows].astype(jnp.int32)
     spot_b = jnp.where(spot, 1.0, 0.0).astype(f32).astype(bf16)
-    spot3 = jnp.concatenate([spot_b] * 3, axis=1)
+    spread_at[...] = jnp.concatenate([spot_b] * 3, axis=1)
 
     def assemble(vals, first, last):
         low = max(0, first - spare) // LANES * LANES
         high = min(child_cols, last)
         spread = dot(vals[:, low:high], hot[first:last, low:high], ((1,), (1,)))
-        front[:, first:last] = front[:, first:last] + dot(spot3, spread.astype(bf16), ((1,), (0,)))
+        front[:, first:last] = front[:, first:last] + dot(spread_at[...], spread.astype(bf16), ((1,), (0,)))
 
     lead_vals = jnp.concatenate(pieces(flat[:, :LANES]), axis=0)
     assemble(lead_vals, 0, PANEL)
@@ -227,51 +227,66 @@
             copy.start()
         panel[...] = front[:, :PANEL]
 
-    @pl.when(col != 0)
-    def _():
-        pan_copies[0].wait_recv()
-
-    block_panel = panel[...]
-    turned = jnp.transpose(block_panel)
-    gram[...] = dot_full(turned, block_panel)
-
     chunks = min(n, PANEL // SUBLANES)
     chunk = PANEL // chunks
     own_chunk = lax.rem(row, chunks)
     own_rows = pl.ds(pl.multiple_of(own_chunk * chunk, SUBLANES), chunk)
-    for code in reversed(range(1, n)):
-        peer = flipped(row, code)
-        start = pl.multiple_of(lax.rem(peer, chunks) * chunk, SUBLANES)
-        pltpu.make_async_remote_copy(
-            src_ref=gram.at[pl.ds(start, chunk)], dst_ref=gram_in.at[row],
-            send_sem=gram_sem.at[0], recv_sem=gram_sem.at[1], device_id=(peer, col), device_id_type=MESH).start()
-    gram_in[row] = gram[own_rows, :]
+
+    def gram_step():
+        turned = jnp.transpose(panel[...])
+        gram[...] = dot_full(turned, panel[...])
+        for code in reversed(range(1, n)):
+            peer = flipped(row, code)
+            start = pl.multiple_of(lax.rem(peer, chunks) * chunk, SUBLANES)
+            pltpu.make_async_remote_copy(
+                src_ref=gram.at[pl.ds(start, chunk)], dst_ref=gram_in.at[row],
+                send_sem=gram_sem.at[0], recv_sem=gram_sem.at[1], device_id=(peer, col), device_id_type=MESH).start()
+        gram_in[row] = gram[own_rows, :]
+        high, low, _ = pieces(turned)
+        turned3[...] = jnp.concatenate([high, high, low], axis=1)
+
+    pl.when(col == 0)(gram_step)
 
     tail_all = landed(tail_in.at[pl.ds(0, n - 1)], tail_sem.at[0], tail_sem.at[1], other)
     tail_all.wait_recv()
     for k in range(n):
         flat[k * block : (k + 1) * block, LANES:] = tail_in[k]
-    vals = jnp.concatenate([lead_vals, jnp.concatenate(pieces(flat[:, LANES:]), axis=0)], axis=1)
-    first = PANEL
-    while first < cols_dev:
-        last = min(cols_dev, (first // TILE + 1) * TILE)
-        assemble(vals, first, last)
-        first = last
-
-    high, low, _ = pieces(turned)
-    turned3 = jnp.concatenate([high, high, low], axis=1)
-    opening = jnp.where(col == 0, sides, front[:, :PANEL])
-
-    def products(first, last):
-        def product(right):
-            top, rest, _ = pieces(right)
-            return dot(turned3, jnp.concatenate([top, rest, top], axis=0), ((1,), (0,)))
-
-        if first == 0:
-            prod[:, :PANEL] = product(opening)
-            first = PANEL
-        if last > first:
-            prod[:, first:last] = product(front[:, first:last])
+    tail_vals = jnp.concatenate(pieces(flat[:, LANES:]), axis=0)
+    stacked[...] = jnp.concatenate([lead_vals, tail_vals], axis=1)
+
+    def assemble_block(first):
+        last = min(cols_dev, first + TILE)
+        assemble(stacked, max(first, PANEL), last)
+
+    @pl.when(col != 0)
+    def _():
+        for first in range(0, cols_dev, TILE):
+            assemble_block(first)
+        pan_copies[0].wait_recv()
+        gram_step()
+
+    block_panel = panel[...]
+
+    def product(right):
+        top, rest, _ = pieces(right)
+        return dot(turned3[...], jnp.concatenate([top, rest, top], axis=0), ((1,), (0,)))
+
+    ready = [0]
+
+    def products(last):
+        while ready[0] < last:
+            first = ready[0]
+            upto = min(cols_dev, first + TILE)
+
+            @pl.when(col == 0)
+            def _():
+                assemble_block(first)
+
+            right = front[:, first:upto]
+            if first == 0:
+                right = jnp.concatenate([jnp.where(col == 0, sides, right[:, :PANEL]), right[:, PANEL:]], axis=1)
+            prod[:, first:upto] = product(right)
+            ready[0] = upto
 
     starts, parts, halving = plan(n, prod.shape[1])
     base = [row * 0] * len(parts)
@@ -351,7 +366,7 @@
 
     marks = [[] for _ in parts]
     at, size = 0, PANEL
-    held, at, size = send_stage(0, at, size, True, lambda q: products(starts[q], starts[q + 1]))
+    held, at, size = send_stage(0, at, size, True, lambda q: products(starts[q + 1]))
 
     gathered = landed(gram_in.at[pl.ds(0, n - 1)], gram_sem.at[0], gram_sem.at[1], other)
     gathered.wait_recv()
@@ -495,6 +510,9 @@
                 pltpu.VMEM((n, block, child_cols - LANES), f32),
                 pltpu.VMEM((n, block, child_cols - LANES), f32),
                 pltpu.VMEM((child_rows, child_cols), f32),
+                pltpu.VMEM((3 * child_rows, child_cols), bf16),
+                pltpu.VMEM((rows_dev, 3 * child_rows), bf16),
+                pltpu.VMEM((PANEL, 3 * rows_dev), bf16),
                 pltpu.VMEM((cols_dev, child_cols), bf16),
                 pltpu.VMEM((PANEL, cols_dev), f32),
                 pltpu.VMEM((nparts, landing_rows, widest), f32),

time: 39.9 us -> 38.2 us (0.957)
  Pallas kernels: 39.1 us -> 37.4 us
    pallas_call x1, Pallas kernels: 37.2 us -> 35.4 us  [shards(): pl.pallas_call(functools.partial(kernel, n, ncols), out_shape=(pltpu.VMEM...]
where the time goes in v3:
time: 38.2 us; the launch traced here: 38 us
  Pallas kernels  37.4 us (98%)
  between operations  0.66 us (2%)
    pallas_call x1, Pallas kernels, shards(): pl.pallas_call(functools.partial(kernel, n, ncols), out_shape=(pltpu.VMEM...  35.4 us
    pallas_call x1, Pallas kernels, shards(): pl.pallas_call(finish, out_shape=(jax.ShapeDtypeStruct((rows_dev, cols_de...  1.94 us

profile of v3, /device:TPU:0, one launch (start us, length us, event | category | flops | bytes accessed | tf_op | source)
XLA Modules:
  0.0 38.0 jit_solution(13877003835346174261)
XLA Ops:
  0.6 0.0 copy-start
  0.6 35.4 %shard_map.85 = (f32[256,1024]{1,0:T(8,128)S(1)}, bf16[256,384]{1,0:T(8,128)(2,1)S(1)}, f32[128,128]{1,0:T(8,128)S(1)}, f32[128,1024]{1,0:T(8,128)S(1)}, f32[128,128]{1,0:T(8,128)S(1)}) custom-call(s32[16]{0:T(128)} %owner_hbm.1, f32[256,1024]{1,0:T(8,128)} %parent.1, f32[64,256]{1,0:T(8,128)} %bitcast.5, f32[64,512]{1,0:T(8,128)} %child_hbm.1, ...), custom_call_target="tpu_custom_call" | custom-call | tf_op jit(solution)/shard_map/pallas_call | solution.py:490
  36.1 0.0 copy-done
  36.1 1.9 %shard_map.86 = (f32[256,1024]{1,0:T(8,128)}, f32[64,128]{1,0:T(8,128)}, f32[64,256]{1,0:T(8,128)}) custom-call(f32[256,1024]{1,0:T(8,128)S(1)} %get-tuple-element.11.front, bf16[256,384]{1,0:T(8,128)(2,1)S(1)} %get-tuple-element.12.left, f32[128,128]{1,0:T(8,128)S(1)} %get-tuple-element.13.inverse, f32[128,1024]{1,0:T(8,128)S(1)} %get-tuple-element.14.total, ...), custom_call_target="tpu_custom_call" | custom-call | tf_op jit(solution)/shard_map/pallas_call | solution.py:535
Async XLA Ops:
  0.6 35.4 %copy-start = (f32[256,64]{0,1:T(8,128)S(1)}, f32[256,64]{0,1:T(8,128)}, u32[]{:S(2)}) copy-start(f32[256,64]{0,1:T(8,128)} %param.7) | copy-start | bytes 196612

commit v4 on v3

--- a/solution.py
+++ b/solution.py
@@ -90,9 +90,10 @@
 
 
 def flipped(index, code):
-    for bit in range(code.bit_length()):
+    moves = [((1 << bit) - 2 * (1 << bit) * ((index // (1 << bit)) % 2)) for bit in range(code.bit_length())]
+    for bit, move in enumerate(moves):
         if code >> bit & 1:
-            index = index + (1 - 2 * ((index // (1 << bit)) % 2)) * (1 << bit)
+            index = index + move
     return index
 
 
@@ -446,9 +447,10 @@
         side_copies[0].wait_recv()
 
 
-def finish(front, left, inverse, total, side, rhs_t, updated, side_t, left_t, stage, sems):
+def finish(front, left, inverse, total, side, rhs_t, updated, side_out, left_out, stage, side_t, left_t, sems):
     nrhs = rhs_t.shape[0]
     tile = stage.shape[2]
+    count = stage.shape[0]
     left = left[...]
 
     def product(right):
@@ -456,15 +458,18 @@
         return dot(left, jnp.concatenate([top, rest, top], axis=0), ((1,), (0,)))
 
     copies = []
-    for t in range(stage.shape[0]):
+    for t in range(count):
         at = slice(t * tile, (t + 1) * tile)
         stage[t] = front[:, at] - product(total[:, at])
-        copy = pltpu.make_async_copy(stage.at[t], updated.at[:, pl.ds(t * tile, tile)], sems.at[t])
-        copy.start()
-        copies.append(copy)
-    sides = side[...]
-    side_t[...] = jnp.transpose(dot_full(inverse[...], sides))[:nrhs]
-    left_t[...] = rhs_t[...] - jnp.transpose(product(sides))[:nrhs]
+        copies.append(pltpu.make_async_copy(stage.at[t], updated.at[:, pl.ds(t * tile, tile)], sems.at[t]))
+        copies[-1].start()
+        if t == 0:
+            sides = side[...]
+            side_t[...] = jnp.transpose(dot_full(inverse[...], sides))[:nrhs]
+            left_t[...] = rhs_t[...] - jnp.transpose(product(sides))[:nrhs]
+            for k, (source, target) in enumerate([(side_t, side_out), (left_t, left_out)]):
+                copies.append(pltpu.make_async_copy(source, target, sems.at[count + k]))
+                copies[-1].start()
     for copy in copies:
         copy.wait()
 
@@ -527,7 +532,7 @@
                 dma((ncols + 1,)),
                 dma((2,)),
                 dma((nparts, 2 * nstages)),
-                dma((2, nparts, max(nextra, 1))),
+                dma((2, nparts, nextra) if nextra else (1,)),
             ],
             compiler_params=pltpu.CompilerParams(collective_id=0, has_side_effects=True, vmem_limit_bytes=VMEM_LIMIT),
         )(*[pltpu.with_memory_space_constraint(value, pltpu.HBM) for value in operands])
@@ -540,10 +545,12 @@
                 jax.ShapeDtypeStruct((nrhs, rows_dev), f32),
             ),
             in_specs=[vmem] * 6,
-            out_specs=(hbm, vmem, vmem),
+            out_specs=(hbm, hbm, hbm),
             scratch_shapes=[
                 pltpu.VMEM((cols_dev // tile, rows_dev, tile), f32),
-                dma((cols_dev // tile,)),
+                pltpu.VMEM((nrhs, PANEL), f32),
+                pltpu.VMEM((nrhs, rows_dev), f32),
+                dma((cols_dev // tile + 2,)),
             ],
             compiler_params=pltpu.CompilerParams(vmem_limit_bytes=VMEM_LIMIT),
         )(front, left, inverse, total, side, rhs_t)

time: 38.2 us -> 37.5 us (0.982)
  Pallas kernels: 37.4 us -> 36.7 us
    pallas_call x1, Pallas kernels: 1.94 us -> 1.38 us  [shards(): pl.pallas_call(finish, out_shape=(jax.ShapeDtypeStruct((rows_dev, cols_de...]
where the time goes in v4:
time: 37.5 us; the launch traced here: 37.3 us
  Pallas kernels  36.7 us (98%)
  between operations  0.66 us (2%)
    pallas_call x1, Pallas kernels, shards(): pl.pallas_call(functools.partial(kernel, n, ncols), out_shape=(pltpu.VMEM...  35.3 us
    pallas_call x1, Pallas kernels, shards(): pl.pallas_call(finish, out_shape=(jax.ShapeDtypeStruct((rows_dev, cols_de...  1.38 us

profile of v4, /device:TPU:0, one launch (start us, length us, event | category | flops | bytes accessed | tf_op | source)
XLA Modules:
  0.0 37.3 jit_solution(8942273022902536263)
XLA Ops:
  0.6 0.0 copy-start
  0.6 35.3 %shard_map.85 = (f32[256,1024]{1,0:T(8,128)S(1)}, bf16[256,384]{1,0:T(8,128)(2,1)S(1)}, f32[128,128]{1,0:T(8,128)S(1)}, f32[128,1024]{1,0:T(8,128)S(1)}, f32[128,128]{1,0:T(8,128)S(1)}) custom-call(s32[16]{0:T(128)} %owner_hbm.1, f32[256,1024]{1,0:T(8,128)} %parent.1, f32[64,256]{1,0:T(8,128)} %bitcast.5, f32[64,512]{1,0:T(8,128)} %child_hbm.1, ...), custom_call_target="tpu_custom_call" | custom-call | tf_op jit(solution)/shard_map/pallas_call | solution.py:495
  35.9 0.0 copy-done
  35.9 1.4 %shard_map.86 = (f32[256,1024]{1,0:T(8,128)}, f32[64,128]{1,0:T(8,128)}, f32[64,256]{1,0:T(8,128)}) custom-call(f32[256,1024]{1,0:T(8,128)S(1)} %get-tuple-element.11.front, bf16[256,384]{1,0:T(8,128)(2,1)S(1)} %get-tuple-element.12.left, f32[128,128]{1,0:T(8,128)S(1)} %get-tuple-element.13.inverse, f32[128,1024]{1,0:T(8,128)S(1)} %get-tuple-element.14.total, ...), custom_call_target="tpu_custom_call" | custom-call | tf_op jit(solution)/shard_map/pallas_call | solution.py:540
Async XLA Ops:
  0.6 35.3 %copy-start = (f32[256,64]{0,1:T(8,128)S(1)}, f32[256,64]{0,1:T(8,128)}, u32[]{:S(2)}) copy-start(f32[256,64]{0,1:T(8,128)} %param.7) | copy-start | bytes 196612

commit v5 on v4

--- a/solution.py
+++ b/solution.py
@@ -129,8 +129,8 @@
 
 
 def kernel(n, ncols, owner_hbm, parent, rhs_hbm, child_hbm, row_map_hbm, col_map_hbm,
-           front, left, inverse, total, side, panel, owner, rhs_t, row_map, col_map, child,
-           lead_out, lead_in, tail_out, tail_in, flat, stacked, spread_at, turned3, hot, prod, halves, gram, gram_in, gram_all,
+           front, left, inverse, side, panel, owner, rhs_t, row_map, col_map, child,
+           lead_out, lead_in, tail_out, tail_in, flat, stacked, spread_at, turned3, hot, prod, total, halves, gram, gram_in, gram_all,
            in_sem, lead_sem, tail_sem, pan_sem, gram_sem, side_sem, send_sem, recv_sem, extra_sem):
     row, col = lax.axis_index("rows"), lax.axis_index("cols")
     rows_dev, cols_dev = front.shape
@@ -412,7 +412,14 @@
 
     inverse[...] = -mat
     high, low, _ = pieces(dot_full(block_panel, -mat))
-    left[...] = jnp.concatenate([high, high, low], axis=1)
+    left3 = jnp.concatenate([high, high, low], axis=1)
+    left[...] = left3
+    @pl.when(col == 0)
+    def _():
+        for copy in pan_copies:
+            copy.wait_send()
+
+    updated_to = 0
     for q in range(len(parts)):
         waiting[q].wait_recv()
         if q == 0:
@@ -429,6 +436,16 @@
                 for copy in side_copies:
                     copy.start()
 
+        upto = starts[q + 1] // TILE * TILE if q < len(parts) - 1 else starts[q + 1]
+        for first in range(updated_to, upto, TILE):
+            last = min(first + TILE, upto)
+            right = total[:, first:last]
+            if first == 0:
+                right = jnp.concatenate([jnp.where(col == 0, gram_all[...], right[:, :PANEL]), right[:, PANEL:]], axis=1)
+            top, rest, _ = pieces(right)
+            front[:, first:last] = front[:, first:last] - dot(left3, jnp.concatenate([top, rest, top], axis=0), ((1,), (0,)))
+        updated_to = upto
+
     lead_all.wait_send()
     tail_all.wait_send()
     gathered.wait_send()
@@ -438,38 +455,32 @@
 
     @pl.when(col == 0)
     def _():
-        for copy in pan_copies + side_copies:
+        for copy in side_copies:
             copy.wait_send()
-        total[:, :PANEL] = gram_all[...]
 
     @pl.when(col != 0)
     def _():
         side_copies[0].wait_recv()
 
 
-def finish(front, left, inverse, total, side, rhs_t, updated, side_out, left_out, stage, side_t, left_t, sems):
-    nrhs = rhs_t.shape[0]
-    tile = stage.shape[2]
-    count = stage.shape[0]
-    left = left[...]
-
-    def product(right):
-        top, rest, _ = pieces(right)
-        return dot(left, jnp.concatenate([top, rest, top], axis=0), ((1,), (0,)))
-
-    copies = []
-    for t in range(count):
-        at = slice(t * tile, (t + 1) * tile)
-        stage[t] = front[:, at] - product(total[:, at])
-        copies.append(pltpu.make_async_copy(stage.at[t], updated.at[:, pl.ds(t * tile, tile)], sems.at[t]))
+def finish(front, left, inverse, side, rhs_t, updated, side_out, left_out, side_t, left_t, sems):
+    nrhs, rows_dev = rhs_t.shape
+    count = sems.shape[0] - 2
+    part = rows_dev // count
+    copies = [
+        pltpu.make_async_copy(front.at[pl.ds(k * part, part)], updated.at[pl.ds(k * part, part)], sems.at[k])
+        for k in range(count)
+    ]
+    for copy in copies:
+        copy.start()
+    sides = side[...]
+    side_t[...] = jnp.transpose(dot_full(inverse[...], sides))[:nrhs]
+    top, rest, _ = pieces(sides)
+    fitted = dot(left[...], jnp.concatenate([top, rest, top], axis=0), ((1,), (0,)))
+    left_t[...] = rhs_t[...] - jnp.transpose(fitted)[:nrhs]
+    for k, (source, target) in enumerate([(side_t, side_out), (left_t, left_out)]):
+        copies.append(pltpu.make_async_copy(source, target, sems.at[count + k]))
         copies[-1].start()
-        if t == 0:
-            sides = side[...]
-            side_t[...] = jnp.transpose(dot_full(inverse[...], sides))[:nrhs]
-            left_t[...] = rhs_t[...] - jnp.transpose(product(sides))[:nrhs]
-            for k, (source, target) in enumerate([(side_t, side_out), (left_t, left_out)]):
-                copies.append(pltpu.make_async_copy(source, target, sems.at[count + k]))
-                copies[-1].start()
     for copy in copies:
         copy.wait()
 
@@ -492,17 +503,16 @@
         hbm = pl.BlockSpec(memory_space=pltpu.HBM)
         rhs_t = right_sides.T
         operands = (block_owner, parent_front, rhs_t, child_values, row_map.reshape(1, -1), col_map.reshape(1, -1))
-        front, left, inverse, total, side = pl.pallas_call(
+        front, left, inverse, side = pl.pallas_call(
             functools.partial(kernel, n, ncols),
             out_shape=(
                 pltpu.VMEM((rows_dev, cols_dev), f32),
                 pltpu.VMEM((rows_dev, 3 * PANEL), bf16),
                 pltpu.VMEM((PANEL, PANEL), f32),
-                pltpu.VMEM((PANEL, cols_dev), f32),
                 pltpu.VMEM((PANEL, LANES), f32),
             ),
             in_specs=[hbm] * 6,
-            out_specs=(vmem,) * 5,
+            out_specs=(vmem,) * 4,
             scratch_shapes=[
                 pltpu.VMEM((rows_dev, PANEL), f32),
                 pltpu.SMEM(block_owner.shape, jnp.int32),
@@ -520,6 +530,7 @@
                 pltpu.VMEM((PANEL, 3 * rows_dev), bf16),
                 pltpu.VMEM((cols_dev, child_cols), bf16),
                 pltpu.VMEM((PANEL, cols_dev), f32),
+                pltpu.VMEM((PANEL, cols_dev), f32),
                 pltpu.VMEM((nparts, landing_rows, widest), f32),
                 pltpu.VMEM((PANEL, PANEL), f32),
                 pltpu.VMEM((n, PANEL // chunks, PANEL), f32),
@@ -536,7 +547,6 @@
             ],
             compiler_params=pltpu.CompilerParams(collective_id=0, has_side_effects=True, vmem_limit_bytes=VMEM_LIMIT),
         )(*[pltpu.with_memory_space_constraint(value, pltpu.HBM) for value in operands])
-        tile = min(TILE, cols_dev)
         updated, side_t, left_t = pl.pallas_call(
             finish,
             out_shape=(
@@ -544,16 +554,15 @@
                 jax.ShapeDtypeStruct((nrhs, PANEL), f32),
                 jax.ShapeDtypeStruct((nrhs, rows_dev), f32),
             ),
-            in_specs=[vmem] * 6,
+            in_specs=[vmem] * 5,
             out_specs=(hbm, hbm, hbm),
             scratch_shapes=[
-                pltpu.VMEM((cols_dev // tile, rows_dev, tile), f32),
                 pltpu.VMEM((nrhs, PANEL), f32),
                 pltpu.VMEM((nrhs, rows_dev), f32),
-                dma((cols_dev // tile + 2,)),
+                dma((6,)),
             ],
             compiler_params=pltpu.CompilerParams(vmem_limit_bytes=VMEM_LIMIT),
-        )(front, left, inverse, total, side, rhs_t)
+        )(front, left, inverse, side, rhs_t)
         return updated, side_t.T, left_t.T
 
     in_specs = (

time: 37.5 us -> 37.5 us (level)
  no operation moved by 1% of the time
where the time goes in v5:
time: 37.5 us; the launch traced here: 37.3 us
  Pallas kernels  36.6 us (98%)
  between operations  0.66 us (2%)
    pallas_call x1, Pallas kernels, shards(): pl.pallas_call(functools.partial(kernel, n, ncols), out_shape=(pltpu.VMEM...  35.6 us
    pallas_call x1, Pallas kernels, shards(): pl.pallas_call(finish, out_shape=(jax.ShapeDtypeStruct((rows_dev, cols_de...  1.04 us

profile of v5, /device:TPU:0, one launch (start us, length us, event | category | flops | bytes accessed | tf_op | source)
XLA Modules:
  0.0 37.3 jit_solution(8241646958584279678)
XLA Ops:
  0.6 0.0 copy-start
  0.6 35.6 %shard_map.85 = (f32[256,1024]{1,0:T(8,128)S(1)}, bf16[256,384]{1,0:T(8,128)(2,1)S(1)}, f32[128,128]{1,0:T(8,128)S(1)}, f32[128,128]{1,0:T(8,128)S(1)}) custom-call(s32[16]{0:T(128)} %owner_hbm.1, f32[256,1024]{1,0:T(8,128)} %parent.1, f32[64,256]{1,0:T(8,128)} %bitcast.5, f32[64,512]{1,0:T(8,128)} %child_hbm.1, s32[1,64]{1,0:T(1,128)} %bitcast.8, ...), custom_call_target="tpu_custom_call" | custom-call | tf_op jit(solution)/shard_map/pallas_call | solution.py:506
  36.2 0.0 copy-done
  36.3 1.0 %shard_map.86 = (f32[256,1024]{1,0:T(8,128)}, f32[64,128]{1,0:T(8,128)}, f32[64,256]{1,0:T(8,128)}) custom-call(f32[256,1024]{1,0:T(8,128)S(1)} %get-tuple-element.10.front, bf16[256,384]{1,0:T(8,128)(2,1)S(1)} %get-tuple-element.11.left, f32[128,128]{1,0:T(8,128)S(1)} %get-tuple-element.12.inverse, f32[128,128]{1,0:T(8,128)S(1)} %get-tuple-element.13.side, ...), custom_call_target="tpu_custom_call" | custom-call | tf_op jit(solution)/shard_map/pallas_call | solution.py:550
Async XLA Ops:
  0.6 35.6 %copy-start = (f32[256,64]{0,1:T(8,128)S(1)}, f32[256,64]{0,1:T(8,128)}, u32[]{:S(2)}) copy-start(f32[256,64]{0,1:T(8,128)} %param.7) | copy-start | bytes 196612
